TPU v7x, 32 devices: a whole 2x2x4 slice. The times are simulated.
32 devices in a mesh: groups: 2 (over y), rows: 4 (over z), blocks: 2 (over x), cols: 2 (over core).
Axes of the slice: x: 2, y: 2, z: 4, core: 2. Of those that a mesh axis runs over, the one named last changes fastest.
Arguments:
- inputs: bfloat16 [4096, 1024], P(('groups', 'rows')), parts along dimension 0, may hold values from -6 to 6
- projection: bfloat16 [1024, 8192], P(None, ('groups', 'blocks', 'cols')), parts along dimension 1, may hold values from -0.1875 to 0.1875
- phases: bfloat16 [8192], P(('groups', 'blocks', 'cols')), parts along dimension 0, may hold values from -3.140625 to 3.140625
- inverse_blocks: float32 [4, 2048, 2048], P(('groups', 'blocks'), 'rows'), parts along dimension 0, as said below
- labels: int32 [4096], P(('groups', 'rows')), parts along dimension 0, may hold values from 0 to 999
- predictions: float32 [4096, 1000], P(('groups', 'rows'), 'cols'), parts along dimension 0, may hold values from -4 to 4
- coefficients: float32 [8192, 1000], P(('groups', 'blocks', 'rows'), 'cols'), parts along dimension 0, may hold values from -3 to 3
Outputs:
- new_coefficients: float32 [8192, 1000], P(('groups', 'blocks', 'rows'), 'cols'), parts along dimension 0
- new_predictions: float32 [4096, 1000], P(('groups', 'rows'), 'cols'), parts along dimension 0
There are 2 independent parts, one for each index of `groups`. A program takes and returns all parts, laid end to end along the dimension named above; each array names one. Nothing has to cross between parts.
Inputs may be any that keep to these rules, and one draw needn't show every extreme that they name: `inverse_blocks`: one dense preconditioner for each feature block.
All inputs are finite; a program needn't handle non-finite values.
Results may differ from a plain program's by a relative error of at most 0.0029.
Values may be sent and summed in bfloat16 or wider, within the bound.
No kernel may reach another device: no remote copies, remote signals or barrier semaphores. Data moves between devices by JAX's collectives and lax.ppermute only.
A program may use at most 64 MiB of HBM per device.

v0:
```python
import jax
import jax.numpy as jnp
from jax import lax
from jax.sharding import PartitionSpec as P

DAMPING = 0.5


def cosine_features(inputs, projection, phases):
    angles = (
        jnp.dot(inputs, projection, preferred_element_type=jnp.float32)
        + phases.astype(jnp.float32)[None, :]
    )
    return jnp.cos(angles).astype(jnp.bfloat16)


def shards(inputs, projection, phases, inverse_blocks, labels, predictions, coefficients):
    out_width = predictions.shape[1]
    classes = lax.axis_index("cols") * out_width + jnp.arange(out_width, dtype=jnp.int32)
    onehot = (labels[:, None] == classes[None, :]).astype(jnp.float32)
    residual = (onehot - predictions).astype(jnp.bfloat16)
    half_features = cosine_features(inputs, projection, phases)
    features_full = lax.all_gather(half_features, "cols", axis=1, tiled=True)
    local_inverse = inverse_blocks[0]
    column_slice = features_full
    own_gradient = lax.psum_scatter(
        lax.dot_general(
            column_slice, residual, (((0,), (0,)), ((), ())), preferred_element_type=jnp.float32
        ),
        "rows",
        scatter_dimension=0,
        tiled=True,
    )
    gradient = lax.all_gather(own_gradient, "rows", axis=0, tiled=True)
    solved = jnp.dot(local_inverse, gradient, precision=lax.Precision.HIGHEST)
    step_update = DAMPING * solved
    new_coefficients = coefficients + step_update
    column_slice = features_full
    contribution = jnp.dot(
        column_slice,
        lax.all_gather(step_update.astype(jnp.bfloat16), "rows", axis=0, tiled=True),
        preferred_element_type=jnp.float32,
    )
    summed = lax.psum(contribution, "blocks")
    return (new_coefficients, predictions + summed)


def solution(mesh):
    return jax.shard_map(
        shards,
        mesh=mesh,
        in_specs=(
            P(("groups", "rows"), None),
            P(None, ("groups", "blocks", "cols")),
            P(("groups", "blocks", "cols")),
            P(("groups", "blocks"), "rows", None),
            P(("groups", "rows")),
            P(("groups", "rows"), "cols"),
            P(("groups", "blocks", "rows"), "cols"),
        ),
        out_specs=(P(("groups", "blocks", "rows"), "cols"), P(("groups", "rows"), "cols")),
        check_vma=False,
    )
```

profile of v0, /device:TPU:0, one launch (start us, length us, event | category | flops | bytes accessed | tf_op | source)
XLA Modules:
  0.0 311.2 jit_solution(1773116370345842166)
XLA Ops:
  7.2 0.0 copy-start
  7.2 0.0 all-gather.4.cloned.1.call-start
  7.2 0.8 convert_element_type.15
  8.0 0.7 copy-done
  8.8 0.0 copy-start.1
  8.8 0.0 copy-start.2
  8.8 9.8 %cosine_convert_fusion = bf16[512,1024]{1,0:T(8,128)(2,1)} fusion(bf16[512,1024]{1,0:T(8,128)(2,1)} %param.7, bf16[1024,1024]{1,0:T(8,128)(2,1)S(1)} %copy-done, f32[1024]{0:T(1024)S(1)} %convert_element_type.15), kind=kOutput, calls=%fused_computation.2 | convolution fusion | flops 1074790400 | bytes 4198400 | tf_op jit(solution)/shard_map/dot_general | solution.py:11
  18.6 0.0 all-gather.4.cloned.1.call-update
  18.6 0.0 reduce-scatter.2.cloned.1.call-start
  18.7 13.4 %all-gather.4.cloned.1.call-done = bf16[512,2048]{1,0:T(8,128)(2,1)} async-done(((bf16[512,1024]{1,0:T(8,128)(2,1)}), bf16[512,2048]{1,0:T(8,128)(2,1)}) %all-gather.4.cloned.1.call-update) | async-done | bytes 2097168 | tf_op jit(solution)/shard_map/all_gather | solution.py:23
  32.1 0.0 copy-done.1
  32.1 0.0 copy-done.2
  32.1 5.0 %fusion.8 = f32[2048,500]{1,0:T(8,128)} fusion(bf16[512,2048]{1,0:T(8,128)(2,1)} %all-gather.4.cloned.1.call-done, f32[512,500]{0,1:T(8,128)S(1)} %copy-done.1, s32[512]{0:T(512)S(1)} %copy-done.2, s32[500]{0:T(512)S(1)} %iota_add_fusion), kind=kOutput, calls=%fused_computation.6 | convolution fusion | flops 1049600000 | bytes 7221200 | tf_op jit(solution)/shard_map/dot_general | solution.py:27
  37.0 0.0 reduce-scatter.2.cloned.1.call-update
  37.0 0.0 all-gather.6.cloned.1.call-start
  37.1 78.0 %reduce-scatter.2.cloned.1.call-done = f32[512,500]{1,0:T(8,128)} async-done(((f32[2048,500]{1,0:T(8,128)}), f32[512,500]{1,0:T(8,128)}) %reduce-scatter.2.cloned.1.call-update) | async-done | bytes 1024016 | tf_op jit(solution)/shard_map/reduce_scatter | solution.py:26
  115.1 0.0 all-gather.6.cloned.1.call-update
  115.2 0.2 all-gather.8.cloned.1.call-start
  115.4 82.7 %all-gather.6.cloned.1.call-done = f32[2048,500]{1,0:T(8,128)} async-done(((f32[512,500]{1,0:T(8,128)}), f32[2048,500]{1,0:T(8,128)}) %all-gather.6.cloned.1.call-update) | async-done | bytes 4096016 | tf_op jit(solution)/shard_map/all_gather | solution.py:34
  198.1 17.2 %fusion.11 = (bf16[512,500]{0,1:T(8,128)(2,1)}, f32[512,500]{0,1:T(8,128)}) fusion(f32[512,500]{0,1:T(8,128)} %param.13, f32[2048,500]{1,0:T(8,128)} %all-gather.6.cloned.1.call-done, f32[1,512,2048]{2,1,0:T(8,128)} %param.10), kind=kOutput, calls=%fused_computation.10 | convolution fusion | flops 6292224000 | bytes 10850304 | tf_op jit(solution)/shard_map/dot_general | solution.py:35
  215.3 0.0 all-gather.8.cloned.1.call-update
  215.3 0.0 all-reduce.2.cloned.1.call-start
  215.4 43.9 %all-gather.8.cloned.1.call-done = bf16[2048,500]{0,1:T(8,128)(2,1)} async-done(((bf16[512,500]{0,1:T(8,128)(2,1)}), bf16[2048,500]{0,1:T(8,128)(2,1)}) %all-gather.8.cloned.1.call-update) | async-done | bytes 2048016 | tf_op jit(solution)/shard_map/all_gather | solution.py:41
  259.3 4.4 %fusion.12 = f32[512,500]{0,1:T(8,128)} fusion(bf16[512,2048]{1,0:T(8,128)(2,1)} %all-gather.4.cloned.1.call-done, bf16[2048,500]{0,1:T(8,128)(2,1)} %all-gather.8.cloned.1.call-done), kind=kOutput, calls=%fused_computation.11 | convolution fusion | flops 1048576000 | bytes 5169152 | tf_op jit(solution)/shard_map/dot_general | solution.py:39
  263.7 0.0 all-reduce.2.cloned.1.call-update
  263.8 38.6 %all-reduce.2.cloned.1.call-done = f32[512,500]{0,1:T(8,128)} async-done(((f32[512,500]{0,1:T(8,128)}), f32[512,500]{0,1:T(8,128)}) %all-reduce.2.cloned.1.call-update) | async-done | bytes 1024016 | tf_op jit(solution)/shard_map/psum | solution.py:44
  302.3 2.4 add.33
  (1 shorter events, 0.0 us)
Async XLA Ops:
  7.2 1.6 copy-start
  7.2 24.9 %all-gather.4.cloned.1.call-start = ((), (), s32[]{:S(2)}) async-start(), calls=%async_computation.1 | async-start | bytes 3145728 | tf_op jit(solution)/shard_map/all_gather | solution.py:23
  8.8 23.3 %copy-start.1 = (f32[512,500]{0,1:T(8,128)S(1)}, f32[512,500]{0,1:T(8,128)}, u32[]{:S(2)}) copy-start(f32[512,500]{0,1:T(8,128)} %param.12) | copy-start | bytes 3072004
  8.8 23.3 %copy-start.2 = (s32[512]{0:T(512)S(1)}, s32[512]{0:T(512)}, u32[]{:S(2)}) copy-start(s32[512]{0:T(512)} %param.11) | copy-start | bytes 6148
  18.6 96.5 %reduce-scatter.2.cloned.1.call-start = ((), (), s32[]{:S(2)}) async-start(), calls=%async_computation.2 | async-start | bytes 5242880 | tf_op jit(solution)/shard_map/reduce_scatter | solution.py:26
  37.0 161.1 %all-gather.6.cloned.1.call-start = ((), (), s32[]{:S(2)}) async-start(), calls=%async_computation.3 | async-start | bytes 5242880 | tf_op jit(solution)/shard_map/all_gather | solution.py:34
  115.2 144.1 %all-gather.8.cloned.1.call-start = ((), (), s32[]{:S(2)}) async-start(), calls=%async_computation.4 | async-start | bytes 2580480 | tf_op jit(solution)/shard_map/all_gather | solution.py:41
  215.3 87.0 %all-reduce.2.cloned.1.call-start = ((), (), s32[]{:S(2)}) async-start(), calls=%async_computation.5 | async-start | bytes 2064384 | tf_op jit(solution)/shard_map/psum | solution.py:44
Sparse Core Ops, SparseCore 0:
  18.7 13.2 all-gather.3
  37.2 77.9 reduce-scatter.1
  116.8 81.2 all-gather.5
  215.4 43.8 all-gather.7
  263.9 38.3 all-reduce.1
where the time goes:
time: 311 us
  waiting for transfers between devices  257 us (83%)
  matrix products  36.4 us (12%)
  between operations  13.8 us (4%)
  other arithmetic  3.21 us (1%)
    all_gather x1, waiting for transfers between devices, shards(): gradient = lax.all_gather(own_gradient, 'rows', axis=0, tiled=True)  82.7 us
    reduce_scatter x1, waiting for transfers between devices, shards(): lax.psum_scatter(lax.dot_general(column_slice, residual, (((0,), (0,)), (...  78 us
    all_gather x1, waiting for transfers between devices, shards(): lax.all_gather(step_update.astype(jnp.bfloat16), 'rows', axis=0, tiled=True)  43.9 us
    psum x1, waiting for transfers between devices, shards(): summed = lax.psum(contribution, 'blocks')  38.6 us
    dot_general x1, matrix products, shards(): solved = jnp.dot(local_inverse, gradient, precision=lax.Precision.HIGHEST)  17.2 us
    all_gather x1, waiting for transfers between devices, shards(): features_full = lax.all_gather(half_features, 'cols', axis=1, tiled=True)  13.4 us
    dot_general x1, matrix products, cosine_features(): jnp.dot(inputs, projection, preferred_element_type=jnp.float32)  9.81 us
  transfers between devices with their start and end apart: 5, of which 5 were waited for; matrix products, arithmetic and copies ran while one was open for 0% of the time, Pallas kernels for 0%

commit v1 on v0

--- a/solution.py
+++ b/solution.py
@@ -41,7 +41,7 @@
         lax.all_gather(step_update.astype(jnp.bfloat16), "rows", axis=0, tiled=True),
         preferred_element_type=jnp.float32,
     )
-    summed = lax.psum(contribution, "blocks")
+    summed = jnp.sum(lax.all_gather(contribution, "blocks"), axis=0)
     return (new_coefficients, predictions + summed)
 
 

time: 311 us -> 314 us (level)
  waiting for transfers between devices: 257 us -> 250 us
  other arithmetic: 3.21 us -> 8.17 us
  local copies, waits for them, and re-layouts: 0.74 us -> 4.73 us
    psum x1 -> x0, waiting for transfers between devices: 38.6 us -> none  [shards(): summed = lax.psum(contribution, 'blocks')]
    all_gather x0 -> x1, waiting for transfers between devices: none -> 31.6 us  [shards(): summed = jnp.sum(lax.all_gather(contribution, 'blocks'), axis=0)]
    reduce_sum x0 -> x1, other arithmetic: none -> 4.97 us  [shards(): summed = jnp.sum(lax.all_gather(contribution, 'blocks'), axis=0)]
    all_gather x0 -> x1, local copies, waits for them, and re-layouts: none -> 3.99 us  [shards(): summed = jnp.sum(lax.all_gather(contribution, 'blocks'), axis=0)]
where the time goes in v1:
time: 314 us; the launch traced here: 313 us
  waiting for transfers between devices  250 us (80%)
  matrix products  36.4 us (12%)
  between operations  13.8 us (4%)
  other arithmetic  8.17 us (3%)
  local copies, waits for them, and re-layouts  4.73 us (2%)
    all_gather x1, waiting for transfers between devices, shards(): gradient = lax.all_gather(own_gradient, 'rows', axis=0, tiled=True)  82.7 us
    reduce_scatter x1, waiting for transfers between devices, shards(): lax.psum_scatter(lax.dot_general(column_slice, residual, (((0,), (0,)), (...  78 us
    all_gather x1, waiting for transfers between devices, shards(): lax.all_gather(step_update.astype(jnp.bfloat16), 'rows', axis=0, tiled=True)  43.7 us
    all_gather x1, waiting for transfers between devices, shards(): summed = jnp.sum(lax.all_gather(contribution, 'blocks'), axis=0)  31.6 us
    dot_general x1, matrix products, shards(): solved = jnp.dot(local_inverse, gradient, precision=lax.Precision.HIGHEST)  17.2 us
    all_gather x1, waiting for transfers between devices, shards(): features_full = lax.all_gather(half_features, 'cols', axis=1, tiled=True)  13.4 us
    dot_general x1, matrix products, cosine_features(): jnp.dot(inputs, projection, preferred_element_type=jnp.float32)  9.81 us
  transfers between devices with their start and end apart: 5, of which 5 were waited for; matrix products, arithmetic and copies ran while one was open for 0% of the time, Pallas kernels for 0%

profile of v1, /device:TPU:0, one launch (start us, length us, event | category | flops | bytes accessed | tf_op | source)
XLA Modules:
  0.0 313.3 jit_solution(4050914878520662651)
XLA Ops:
  7.2 0.0 copy-start
  7.2 0.0 all-gather.6.cloned.1.call-start
  7.2 0.8 convert_element_type.15
  8.0 0.7 copy-done
  8.8 0.0 copy-start.1
  8.8 0.0 copy-start.2
  8.8 9.8 %cosine_convert_fusion = bf16[512,1024]{1,0:T(8,128)(2,1)} fusion(bf16[512,1024]{1,0:T(8,128)(2,1)} %param.7, bf16[1024,1024]{1,0:T(8,128)(2,1)S(1)} %copy-done, f32[1024]{0:T(1024)S(1)} %convert_element_type.15), kind=kOutput, calls=%fused_computation.2 | convolution fusion | flops 1074790400 | bytes 4198400 | tf_op jit(solution)/shard_map/dot_general | solution.py:11
  18.6 0.0 all-gather.6.cloned.1.call-update
  18.6 0.0 reduce-scatter.2.cloned.1.call-start
  18.7 13.4 %all-gather.6.cloned.1.call-done = bf16[512,2048]{1,0:T(8,128)(2,1)} async-done(((bf16[512,1024]{1,0:T(8,128)(2,1)}), bf16[512,2048]{1,0:T(8,128)(2,1)}) %all-gather.6.cloned.1.call-update) | async-done | bytes 2097168 | tf_op jit(solution)/shard_map/all_gather | solution.py:23
  32.1 0.0 copy-done.1
  32.1 0.0 copy-done.2
  32.1 5.0 %fusion.8 = f32[2048,500]{1,0:T(8,128)} fusion(bf16[512,2048]{1,0:T(8,128)(2,1)} %all-gather.6.cloned.1.call-done, f32[512,500]{0,1:T(8,128)S(1)} %copy-done.1, s32[512]{0:T(512)S(1)} %copy-done.2, s32[500]{0:T(512)S(1)} %iota_add_fusion), kind=kOutput, calls=%fused_computation.6 | convolution fusion | flops 1049600000 | bytes 7221200 | tf_op jit(solution)/shard_map/dot_general | solution.py:27
  37.0 0.0 reduce-scatter.2.cloned.1.call-update
  37.0 0.0 all-gather.8.cloned.1.call-start
  37.1 78.0 %reduce-scatter.2.cloned.1.call-done = f32[512,500]{1,0:T(8,128)} async-done(((f32[2048,500]{1,0:T(8,128)}), f32[512,500]{1,0:T(8,128)}) %reduce-scatter.2.cloned.1.call-update) | async-done | bytes 1024016 | tf_op jit(solution)/shard_map/reduce_scatter | solution.py:26
  115.1 0.0 all-gather.8.cloned.1.call-update
  115.2 0.2 all-gather.10.cloned.1.call-start
  115.4 82.7 %all-gather.8.cloned.1.call-done = f32[2048,500]{1,0:T(8,128)} async-done(((f32[512,500]{1,0:T(8,128)}), f32[2048,500]{1,0:T(8,128)}) %all-gather.8.cloned.1.call-update) | async-done | bytes 4096016 | tf_op jit(solution)/shard_map/all_gather | solution.py:34
  198.1 17.2 %fusion.11 = (bf16[512,500]{0,1:T(8,128)(2,1)}, f32[512,500]{0,1:T(8,128)}) fusion(f32[512,500]{0,1:T(8,128)} %param.13, f32[2048,500]{1,0:T(8,128)} %all-gather.8.cloned.1.call-done, f32[1,512,2048]{2,1,0:T(8,128)} %param.10), kind=kOutput, calls=%fused_computation.10 | convolution fusion | flops 6292224000 | bytes 10850304 | tf_op jit(solution)/shard_map/dot_general | solution.py:35
  215.3 0.0 all-gather.10.cloned.1.call-update
  215.3 0.3 all-gather.12.cloned.1.call-start
  215.6 43.7 %all-gather.10.cloned.1.call-done = bf16[2048,500]{0,1:T(8,128)(2,1)} async-done(((bf16[512,500]{0,1:T(8,128)(2,1)}), bf16[2048,500]{0,1:T(8,128)(2,1)}) %all-gather.10.cloned.1.call-update) | async-done | bytes 2048016 | tf_op jit(solution)/shard_map/all_gather | solution.py:41
  259.3 4.4 %fusion.12 = f32[512,500]{0,1:T(8,128)} fusion(bf16[512,2048]{1,0:T(8,128)(2,1)} %all-gather.6.cloned.1.call-done, bf16[2048,500]{0,1:T(8,128)(2,1)} %all-gather.10.cloned.1.call-done), kind=kOutput, calls=%fused_computation.11 | convolution fusion | flops 1048576000 | bytes 5169152 | tf_op jit(solution)/shard_map/dot_general | solution.py:39
  263.7 0.0 all-gather.12.cloned.1.call-update
  263.8 31.6 %all-gather.12.cloned.1.call-done = f32[1024,500]{0,1:T(8,128)} async-done(((f32[512,500]{0,1:T(8,128)}), f32[1024,500]{0,1:T(8,128)}) %all-gather.12.cloned.1.call-update) | async-done | bytes 2048016 | tf_op jit(solution)/shard_map/all_gather | solution.py:44
  295.4 4.0 %reshape.10 = f32[2,512,500]{1,0,2:T(2,128)} reshape(f32[1024,500]{0,1:T(8,128)} %all-gather.12.cloned.1.call-done) | data formatting | bytes 4096000 | tf_op jit(solution)/shard_map/all_gather | solution.py:44
  299.4 5.0 %reduce_sum.9 = f32[512,500]{0,1:T(8,128)} reduce(f32[2,512,500]{1,0,2:T(2,128)} %reshape.10, f32[]{:T(128)} %constant.3.clone.1), dimensions={0}, to_apply=%region_1.0 | reduce | flops 256000 | bytes 3072004 | tf_op jit(solution)/shard_map/reduce_sum | solution.py:44
  304.3 2.4 add.31
  (1 shorter events, 0.0 us)
Async XLA Ops:
  7.2 1.6 copy-start
  7.2 24.9 %all-gather.6.cloned.1.call-start = ((), (), s32[]{:S(2)}) async-start(), calls=%async_computation.1 | async-start | bytes 3145728 | tf_op jit(solution)/shard_map/all_gather | solution.py:23
  8.8 23.3 %copy-start.1 = (f32[512,500]{0,1:T(8,128)S(1)}, f32[512,500]{0,1:T(8,128)}, u32[]{:S(2)}) copy-start(f32[512,500]{0,1:T(8,128)} %param.12) | copy-start | bytes 3072004
  8.8 23.3 %copy-start.2 = (s32[512]{0:T(512)S(1)}, s32[512]{0:T(512)}, u32[]{:S(2)}) copy-start(s32[512]{0:T(512)} %param.11) | copy-start | bytes 6148
  18.6 96.5 %reduce-scatter.2.cloned.1.call-start = ((), (), s32[]{:S(2)}) async-start(), calls=%async_computation.2 | async-start | bytes 5242880 | tf_op jit(solution)/shard_map/reduce_scatter | solution.py:26
  37.0 161.1 %all-gather.8.cloned.1.call-start = ((), (), s32[]{:S(2)}) async-start(), calls=%async_computation.3 | async-start | bytes 5242880 | tf_op jit(solution)/shard_map/all_gather | solution.py:34
  115.2 144.1 %all-gather.10.cloned.1.call-start = ((), (), s32[]{:S(2)}) async-start(), calls=%async_computation.4 | async-start | bytes 2580480 | tf_op jit(solution)/shard_map/all_gather | solution.py:41
  215.3 80.1 %all-gather.12.cloned.1.call-start = ((), (), s32[]{:S(2)}) async-start(), calls=%async_computation.5 | async-start | bytes 3096576 | tf_op jit(solution)/shard_map/all_gather | solution.py:44
Sparse Core Ops, SparseCore 0:
  18.7 13.2 all-gather.5
  37.2 77.9 reduce-scatter.1
  116.8 81.2 all-gather.7
  215.4 43.8 all-gather.9
  263.9 31.4 all-gather.11
